TPU v7x, 128 devices: a whole 4x4x4 slice. The times are simulated.
128 devices in a mesh: dp: 16 (over y, x), expert: 4 (over z), tensor: 2 (over core).
Axes of the slice: x: 4, y: 4, z: 4, core: 2. Of those that a mesh axis runs over, the one named last changes fastest.
Arguments:
- tokens: bfloat16 [8192, 2048], P(('dp', 'expert')), may hold values from -6 to 6
- expert_ids: int32 [8192, 2], P(('dp', 'expert')), may hold values from 0 to 3, all different within a row; in each aligned block of 128 rows (0 to 127, 128 to 255, ...) at most 96 rows name the same one
- gate_values: float32 [8192, 2], P(('dp', 'expert')), may hold values from 0.1 to 1
- tag_labels: int32 [8192], P(('dp', 'expert')), may hold values from 0 to 31
- w_gate: bfloat16 [4, 2048, 7168], P('expert', 'dp', 'tensor'), may hold values from -0.125 to 0.125
- w_up: bfloat16 [4, 2048, 7168], P('expert', 'dp', 'tensor'), may hold values from -0.125 to 0.125
- w_down: bfloat16 [4, 7168, 2048], P('expert', 'tensor', 'dp'), may hold values from -0.0625 to 0.0625
- adapter_in: bfloat16 [4, 16, 2048], P('expert'), may hold values from -0.125 to 0.125
- adapter_out: bfloat16 [4, 16, 7168], P('expert', None, 'tensor'), may hold values from -1.5 to 1.5
- tag_weight: bfloat16 [2048, 32], replicated, may hold values from -0.125 to 0.125
Outputs:
- layer_out: bfloat16 [8192, 2048], P(('dp', 'expert'), 'tensor')
- in_gradient: float32 [4, 16, 2048], P('expert')
- out_gradient: float32 [4, 16, 7168], P('expert', None, 'tensor')
Inputs may be any that keep to these rules, and one draw needn't show every extreme that they name: `expert_ids`: each row names 2 different experts; the rows of one index of dp and expert name each expert at most 96 times, a bound that some block reaches.
All inputs are finite; a program needn't handle non-finite values.
Results may differ from a plain program's by a relative error of at most 0.017.
Values may be sent and summed in bfloat16 or wider, within the bound.
A program may use at most 128 MiB of HBM per device.

v0:
```python
import jax
import jax.numpy as jnp
from jax import lax
from jax.sharding import PartitionSpec as P

adapter_scale = 2.0


def contract_last(left, right):
    return lax.dot_general(
        left, right, (((1,), (1,)), ((), ())), preferred_element_type=jnp.float32
    )


def contract_first(left, right):
    return lax.dot_general(
        left, right, (((0,), (0,)), ((), ())), preferred_element_type=jnp.float32
    )


def tag_gradient(logits, tag_labels):
    exp_logits = jnp.exp(logits)
    probability = exp_logits / jnp.sum(exp_logits, axis=1, keepdims=True)
    labels_hot = (
        tag_labels[:, None] == jnp.arange(logits.shape[1], dtype=jnp.int32)[None, :]
    ).astype(jnp.float32)
    return probability - labels_hot


def local(
    tokens,
    expert_ids,
    gate_values,
    tag_labels,
    w_gate,
    w_up,
    w_down,
    adapter_in,
    adapter_out,
    tag_weight,
):
    experts = lax.axis_size("expert")
    shards = lax.axis_size("tensor")
    tok_count = tokens.shape[0]
    model_width = tokens.shape[1]
    share_width = model_width // shards
    capacity = 3 * tok_count // experts
    slot_count = experts * capacity
    flat_ids = expert_ids.reshape(-1)
    onehot = (flat_ids[:, None] == jnp.arange(experts, dtype=jnp.int32)[None, :]).astype(jnp.int32)
    before = jnp.cumsum(onehot, axis=0) - onehot
    position = jnp.sum(before * onehot, axis=1)
    slot_index = (flat_ids * capacity + position).reshape(tok_count, expert_ids.shape[1])
    matches = jnp.arange(slot_count, dtype=jnp.int32)[:, None, None] == slot_index[None, :, :]
    dispatch = jnp.sum(matches.astype(jnp.float32), axis=2).astype(jnp.bfloat16)
    combine = jnp.sum(jnp.where(matches, gate_values[None, :, :], jnp.float32(0.0)), axis=2).T
    outgoing = jnp.dot(dispatch, tokens, preferred_element_type=jnp.float32).astype(jnp.bfloat16)
    arrived = lax.all_to_all(
        outgoing.reshape(experts, capacity, model_width),
        "expert",
        split_axis=0,
        concat_axis=0,
        tiled=True,
    ).reshape(slot_count, model_width)
    gate_acc = jnp.dot(
        arrived,
        lax.all_gather(w_gate, "dp", axis=1, tiled=True)[0],
        preferred_element_type=jnp.float32,
    )
    up_acc = jnp.dot(
        arrived,
        lax.all_gather(w_up, "dp", axis=1, tiled=True)[0],
        preferred_element_type=jnp.float32,
    )
    low_rank = contract_last(arrived, adapter_in[0]).astype(jnp.bfloat16)
    up_full = up_acc + adapter_scale * jnp.dot(
        low_rank, adapter_out[0], preferred_element_type=jnp.float32
    )
    activated = jax.nn.silu(gate_acc)
    hidden = (activated * up_full).astype(jnp.bfloat16)
    down_full = lax.all_gather(w_down, "dp", axis=2, tiled=True)[0]
    partial_value = jnp.dot(hidden, down_full, preferred_element_type=jnp.float32)
    column_start = lax.axis_index("tensor") * share_width
    summed = lax.psum(partial_value, "tensor").astype(jnp.bfloat16)
    returned = lax.all_to_all(
        summed.reshape(experts, capacity, model_width),
        "expert",
        split_axis=0,
        concat_axis=0,
        tiled=True,
    ).reshape(slot_count, model_width)
    mixed_rows = tokens.astype(jnp.float32) + jnp.dot(
        combine, returned.astype(jnp.float32), precision=lax.Precision.HIGHEST
    )
    layer_full = mixed_rows.astype(jnp.bfloat16)
    logits = jnp.dot(layer_full, tag_weight, preferred_element_type=jnp.float32)
    logit_grad = tag_gradient(logits, tag_labels)
    upstream = jnp.dot(
        logit_grad, tag_weight.astype(jnp.float32).T, precision=lax.Precision.HIGHEST
    )
    slot_out = jnp.dot(combine.T, upstream, precision=lax.Precision.HIGHEST).astype(jnp.bfloat16)
    slot_grad = lax.all_to_all(
        slot_out.reshape(experts, capacity, model_width),
        "expert",
        split_axis=0,
        concat_axis=0,
        tiled=True,
    ).reshape(slot_count, model_width)
    layer_out = lax.dynamic_slice_in_dim(layer_full, column_start, share_width, 1)
    hidden_grad = contract_last(slot_grad, down_full)
    up_grad = (hidden_grad * activated).astype(jnp.bfloat16)
    out_local = adapter_scale * contract_first(low_rank, up_grad)
    low_grad = adapter_scale * contract_last(up_grad, adapter_out[0])
    in_local = lax.dot_general(
        low_grad,
        arrived.astype(jnp.float32),
        (((0,), (0,)), ((), ())),
        precision=lax.Precision.HIGHEST,
    )
    in_total = lax.psum(in_local.astype(jnp.bfloat16), ("dp", "tensor")).astype(jnp.float32)
    out_total = lax.psum(out_local.astype(jnp.bfloat16), "dp").astype(jnp.float32)
    return (layer_out, in_total[None], out_total[None])


def solution(mesh):
    in_specs = (
        P(("dp", "expert"), None),
        P(("dp", "expert"), None),
        P(("dp", "expert"), None),
        P(("dp", "expert")),
        P("expert", "dp", "tensor"),
        P("expert", "dp", "tensor"),
        P("expert", "tensor", "dp"),
        P("expert", None, None),
        P("expert", None, "tensor"),
        P(),
    )
    out_specs = (
        P(("dp", "expert"), "tensor"),
        P("expert", None, None),
        P("expert", None, "tensor"),
    )
    return jax.shard_map(local, mesh=mesh, in_specs=in_specs, out_specs=out_specs, check_vma=False)
```

profile of v0, /device:TPU:1, one launch (start us, length us, event | category | flops | bytes accessed | tf_op | source)
XLA Modules:
  0.0 609.7 jit_solution(16985919612496595279)
XLA Ops:
  7.2 0.7 all-gather.6.cloned.1.call-update
  8.0 0.7 all-gather.4.cloned.1.call-update
  8.7 0.7 all-gather.8.cloned.1.call-update
  9.4 0.8 copy.31
  10.5 1.2 reduce-window.6
  12.4 0.7 multiply_add_fusion
  13.1 0.8 convert_reduce_fusion
  13.9 0.6 convolution_convert_fusion.1
  14.4 25.5 %all_to_all.15 = bf16[4,96,2048]{2,1,0:T(8,128)(2,1)S(1)} all-to-all(bf16[4,96,2048]{2,1,0:T(8,128)(2,1)S(1)} %bitcast.78), channel_id=1, replica_groups=mesh['dp'=16,'expert'=4,'tensor'=2] {'expert'}, dimensions={0} | all-to-all | bytes 3145728 | tf_op jit(solution)/shard_map/all_to_all | solution.py:58
  40.5 73.1 %all-gather.6.cloned.1.call-done = bf16[1,2048,3584]{2,1,0:T(8,128)(2,1)} async-done(((bf16[1,128,3584]{2,1,0:T(8,128)(2,1)}), bf16[1,2048,3584]{2,1,0:T(8,128)(2,1)}) %all-gather.6.cloned.1.call-update) | async-done | bytes 14680080 | tf_op jit(solution)/shard_map/all_gather | solution.py:72
  113.6 11.5 %fusion.4 = f32[384,3584]{1,0:T(8,128)} fusion(bf16[384,2048]{1,0:T(8,128)(2,1)S(1)} %bitcast.75, bf16[1,2048,3584]{2,1,0:T(8,128)(2,1)} %all-gather.6.cloned.1.call-done), kind=kOutput, calls=%fused_computation.4 | convolution fusion | flops 5637144576 | bytes 21757952 | tf_op jit(solution)/shard_map/dot_general | solution.py:70
  125.1 90.7 %all-gather.4.cloned.1.call-done = bf16[1,2048,3584]{2,1,0:T(8,128)(2,1)} async-done(((bf16[1,128,3584]{2,1,0:T(8,128)(2,1)}), bf16[1,2048,3584]{2,1,0:T(8,128)(2,1)}) %all-gather.4.cloned.1.call-update) | async-done | bytes 14680080 | tf_op jit(solution)/shard_map/all_gather | solution.py:67
  215.8 11.1 %divide_multiply_fusion = f32[384,3584]{1,0:T(8,128)} fusion(bf16[384,2048]{1,0:T(8,128)(2,1)S(1)} %bitcast.76, bf16[1,2048,3584]{2,1,0:T(8,128)(2,1)} %all-gather.4.cloned.1.call-done), kind=kOutput, calls=%fused_computation.14 | convolution fusion | flops 5642649600 | bytes 21757952 | tf_op jit(solution)/shard_map/dot_general | solution.py:65
  226.9 98.6 %all-gather.8.cloned.1.call-done = bf16[1,3584,2048]{2,1,0:T(8,128)(2,1)} async-done(((bf16[1,3584,128]{2,1,0:T(8,128)(2,1)}), bf16[1,3584,2048]{2,1,0:T(8,128)(2,1)}) %all-gather.8.cloned.1.call-update) | async-done | bytes 14680080 | tf_op jit(solution)/shard_map/all_gather | solution.py:81
  325.5 15.2 %fusion.2 = f32[384,2048]{1,0:T(8,128)} fusion(bf16[1,3584,2048]{2,1,0:T(8,128)(2,1)} %all-gather.8.cloned.1.call-done, f32[384,3584]{1,0:T(8,128)} %divide_multiply_fusion, f32[384,3584]{1,0:T(8,128)} %fusion.4, bf16[384,16]{0,1:T(8,128)(2,1)S(1)} %convolution_convert_fusion.3, bf16[1,16,3584]{2,1,0:T(8,128)(2,1)S(1)} %copy-done.4), kind=kOutput, calls=%fused_computation.2 | convolution fusion | flops 5686689792 | bytes 28962816 | tf_op jit(solution)/shard_map/dot_general | solution.py:82
  340.7 14.1 %all-reduce.7 = bf16[384,2048]{1,0:T(8,128)(2,1)S(1)} all-reduce(f32[384,2048]{1,0:T(8,128)} %fusion.2), channel_id=1, replica_groups=mesh['dp'=16,'expert'=4,'tensor'=2] {'tensor'}, use_global_device_ids=true, to_apply=%region_5.6 | all-reduce | flops 786432 | bytes 4718592 | tf_op jit(solution)/shard_map/psum | solution.py:84
  354.8 24.3 %all_to_all.16 = bf16[4,96,2048]{2,1,0:T(8,128)(2,1)S(1)} all-to-all(bf16[4,96,2048]{2,1,0:T(8,128)(2,1)S(1)} %bitcast.80), channel_id=1, replica_groups=mesh['dp'=16,'expert'=4,'tensor'=2] {'expert'}, dimensions={0} | all-to-all | bytes 3145728 | tf_op jit(solution)/shard_map/all_to_all | solution.py:85
  379.2 1.0 fusion.21
  380.5 0.6 fusion.28
  381.2 3.7 convolution_convert_fusion
  384.9 4.4 all-to-all-start.2
  389.3 19.5 %all-to-all-done.2 = bf16[4,96,2048]{2,1,0:T(8,128)(2,1)} async-done(((bf16[4,96,2048]{2,1,0:T(8,128)(2,1)}), bf16[4,96,2048]{2,1,0:T(8,128)(2,1)}, u32[]{:S(2)}, u32[]{:S(2)}) %all-to-all-start.2) | async-done | bytes 1572896 | tf_op jit(solution)/shard_map/all_to_all | solution.py:102
  408.8 10.4 %fusion.13 = bf16[384,3584]{1,0:T(8,128)(2,1)S(1)} fusion(f32[384,3584]{1,0:T(8,128)} %divide_multiply_fusion, bf16[384,2048]{1,0:T(8,128)(2,1)} %bitcast.12, bf16[1,3584,2048]{2,1,0:T(8,128)(2,1)} %all-gather.8.cloned.1.call-done), kind=kOutput, calls=%fused_computation.12 | convolution fusion | flops 5639897088 | bytes 24510464 | tf_op jit(solution)/shard_map/dot_general | solution.py:10
  419.3 0.8 convolution_multiply_fusion.2
  420.1 0.6 copy-done.2
  420.7 1.4 fusion.22
  422.1 1.1 fusion.20
  423.3 0.7 constant_dynamic-slice_fusion
  424.0 94.4 %all-reduce.4.cloned.1.call-done = bf16[1,16,2048]{2,1,0:T(8,128)(2,1)} async-done(((bf16[1,16,2048]{2,1,0:T(8,128)(2,1)}), bf16[1,16,2048]{2,1,0:T(8,128)(2,1)}) %all-reduce.4.cloned.1.call-update) | async-done | bytes 65552 | tf_op jit(solution)/shard_map/psum | solution.py:120
  518.3 1.5 broadcast_in_dim.33
  519.8 81.7 %all-reduce.6.cloned.1.call-done = bf16[1,16,3584]{2,1,0:T(8,128)(2,1)} async-done(((bf16[1,16,3584]{2,1,0:T(8,128)(2,1)}), bf16[1,16,3584]{2,1,0:T(8,128)(2,1)}) %all-reduce.6.cloned.1.call-update) | async-done | bytes 114704 | tf_op jit(solution)/shard_map/psum | solution.py:121
  601.6 1.6 broadcast_in_dim.35
  (34 shorter events, 2.0 us)
Async XLA Ops:
  7.2 373.0 %copy-start = (bf16[2048,32]{0,1:T(8,128)(2,1)S(1)}, bf16[2048,32]{0,1:T(8,128)(2,1)}, u32[]{:S(2)}) copy-start(bf16[2048,32]{0,1:T(8,128)(2,1)} %param.19) | copy-start | bytes 393220
  7.2 6.7 %copy-start.3 = (bf16[128,2048]{1,0:T(8,128)(2,1)S(1)}, bf16[128,2048]{1,0:T(8,128)(2,1)}, u32[]{:S(2)}) copy-start(bf16[128,2048]{1,0:T(8,128)(2,1)} %param.10) | copy-start | bytes 1572868
  7.2 106.4 %all-gather.6.cloned.1.call-start = ((), (), s32[]{:S(2)}) async-start(), calls=%async_computation.4 | async-start | bytes 15597568 | tf_op jit(solution)/shard_map/all_gather | solution.py:72
  7.9 207.9 %all-gather.4.cloned.1.call-start = ((), (), s32[]{:S(2)}) async-start(), calls=%async_computation.3 | async-start | bytes 15597568 | tf_op jit(solution)/shard_map/all_gather | solution.py:67
  8.7 316.8 %all-gather.8.cloned.1.call-start = ((), (), s32[]{:S(2)}) async-start(), calls=%async_computation.5 | async-start | bytes 15597568 | tf_op jit(solution)/shard_map/all_gather | solution.py:81
  9.4 30.5 %copy-start.5 = (bf16[1,16,2048]{2,1,0:T(8,128)(2,1)S(1)}, bf16[1,16,2048]{2,1,0:T(8,128)(2,1)}, u32[]{:S(2)}) copy-start(bf16[1,16,2048]{2,1,0:T(8,128)(2,1)} %param.17) | copy-start | bytes 196612
  39.9 175.9 %copy-start.1 = (bf16[4,96,2048]{2,1,0:T(8,128)(2,1)}, bf16[4,96,2048]{2,1,0:T(8,128)(2,1)S(1)}, u32[]{:S(2)}) copy-start(bf16[4,96,2048]{2,1,0:T(8,128)(2,1)S(1)} %all_to_all.15) | copy-start | bytes 4718596
  125.1 200.4 %copy-start.4 = (bf16[1,16,3584]{2,1,0:T(8,128)(2,1)S(1)}, bf16[1,16,3584]{2,1,0:T(8,128)(2,1)}, u32[]{:S(2)}) copy-start(bf16[1,16,3584]{2,1,0:T(8,128)(2,1)} %param.18) | copy-start | bytes 344068
  354.8 25.7 %copy-start.6 = (s32[128]{0:T(128)S(1)}, s32[128]{0:T(128)}, u32[]{:S(2)}) copy-start(s32[128]{0:T(128)} %param.13) | copy-start | bytes 1540
  384.9 24.0 %all-to-all-start.2 = ((bf16[4,96,2048]{2,1,0:T(8,128)(2,1)}), bf16[4,96,2048]{2,1,0:T(8,128)(2,1)}, u32[]{:S(2)}, u32[]{:S(2)}) async-start(bf16[4,96,2048]{2,1,0:T(8,128)(2,1)} %bitcast.11), calls=%async_computation.2 | async-start | bytes 3145728 | tf_op jit(solution)/shard_map/all_to_all | solution.py:102
  389.2 129.1 %all-reduce.4.cloned.1.call-start = ((), (), s32[]{:S(2)}) async-start(), calls=%async_computation.6 | async-start | bytes 131072 | tf_op jit(solution)/shard_map/psum | solution.py:120
  419.3 1.4 copy-start.2
  422.1 179.5 %all-reduce.6.cloned.1.call-start = ((), (), s32[]{:S(2)}) async-start(), calls=%async_computation.7 | async-start | bytes 229376 | tf_op jit(solution)/shard_map/psum | solution.py:121
Sparse Core Ops, SparseCore 0:
  10.1 103.3 all-gather.5
  115.7 100.0 all-gather.3
  217.9 107.4 all-gather.7
  422.2 96.1 all-reduce.3
  522.0 79.5 all-reduce.5
where the time goes:
time: 611 us; the launch traced here: 610 us
  waiting for transfers between devices  460 us (75%)
  blocking collectives  64 us (10%)
  matrix products  58.3 us (10%)
  between operations  13.9 us (2%)
    all_gather x1, waiting for transfers between devices, local(): down_full = lax.all_gather(w_down, 'dp', axis=2, tiled=True)[0]  98.6 us
    psum x1, waiting for transfers between devices, local(): lax.psum(in_local.astype(jnp.bfloat16), ('dp', 'tensor'))  94.4 us
    all_gather x1, waiting for transfers between devices, local(): lax.all_gather(w_gate, 'dp', axis=1, tiled=True)[0]  90.7 us
    psum x1, waiting for transfers between devices, local(): lax.psum(out_local.astype(jnp.bfloat16), 'dp').astype(jnp.float32)  81.7 us
    all_gather x1, waiting for transfers between devices, local(): lax.all_gather(w_up, 'dp', axis=1, tiled=True)[0]  73.1 us
    all_to_all x1, blocking collectives, local(): lax.all_to_all(outgoing.reshape(experts, capacity, model_width), 'expert'...  25.5 us
    all_to_all x1, blocking collectives, local(): lax.all_to_all(summed.reshape(experts, capacity, model_width), 'expert',...  24.3 us
    all_to_all x1, waiting for transfers between devices, local(): lax.all_to_all(slot_out.reshape(experts, capacity, model_width), 'expert'...  19.5 us
  transfers between devices with their start and end apart: 6, of which 6 were waited for; matrix products, arithmetic and copies ran while one was open for 5% of the time, Pallas kernels for 0%

commit v1 on v0

v1 whole, which is shorter than its diff:
```python
import jax
import jax.numpy as jnp
from jax import lax
from jax.experimental import pallas as pl
from jax.experimental.pallas import tpu as pltpu
from jax.sharding import PartitionSpec as P

MESH = pl.DeviceIdType.MESH
BF = jnp.bfloat16
F32 = jnp.float32
EXACT = lax.Precision.HIGHEST

SIDE = 4
DIM = 2048
HALF = 1024
LANE = 128
SHARD = 3584
FQ = 896
RANK = 16
TAGS = 32
TOK = 128
CAP = 96
BLOCK = SIDE * CAP
ROWS = SIDE * BLOCK
TILE = 512


def nn(a, b):
    return lax.dot_general(a, b, (((1,), (0,)), ((), ())), preferred_element_type=F32)


def nt(a, b):
    return lax.dot_general(a, b, (((1,), (1,)), ((), ())), preferred_element_type=F32)


def tn(a, b):
    return lax.dot_general(a, b, (((0,), (0,)), ((), ())), preferred_element_type=F32)


def split(v):
    high = v.astype(BF)
    return high, (v - high.astype(F32)).astype(BF)


def kernel(
    ids_ref, gates_ref, labels_ref, tok_ref, ain_ref, aout_ref, tag_ref, wg_hbm, wu_hbm, wd_hbm,
    layer_ref, ing_ref, outg_ref,
    wg, wu, wd, tsend, xs, act, hid, low, dmat, cmat, own, oth, prt, rss, rsr, zs, ret,
    lgs, lgr, tag4, mp, gs, gx, ingp, fp, fx, ox, fy, oy, done, sem,
):
    me = lax.axis_index("dp")
    y = me // SIDE
    x = lax.rem(me, SIDE)
    z = lax.axis_index("expert")
    c = lax.axis_index("tensor")

    def at(v, d):
        return lax.rem(v + d + SIDE, SIDE)

    def dev(dx=0, dy=0, dz=0, dc=0):
        return (
            at(y, dy) * SIDE + at(x, dx),
            at(z, dz),
            lax.rem(c + dc, 2),
        )

    taken = [0]
    sent = []

    def send(src, dst, to):
        k = taken[0]
        taken[0] += 2
        copy = pltpu.make_async_remote_copy(
            src_ref=src, dst_ref=dst, send_sem=sem.at[k], recv_sem=sem.at[k + 1],
            device_id=to, device_id_type=MESH,
        )
        copy.start()
        sent.append(copy)
        return copy

    barrier = pltpu.get_barrier_semaphore()
    peers = [dev(dc=1)]
    for d in range(1, SIDE):
        peers += [dev(dx=d), dev(dy=d), dev(dz=d)]
    for peer in peers:
        pl.semaphore_signal(barrier, inc=1, device_id=peer, device_id_type=MESH)
    pl.semaphore_wait(barrier, len(peers))

    bufs = (wg, wu, wd)

    def piece(w, q):
        start = pl.multiple_of(q * FQ, LANE)
        if w == 2:
            return wd_hbm.at[0, pl.ds(start, FQ), :]
        return (wg_hbm, wu_hbm)[w].at[0, :, pl.ds(start, FQ)]

    locals_ = []
    first = [[None] * SIDE for _ in range(3)]
    ring = [[[None, None] for _ in range(SIDE)] for _ in range(3)]
    relay = [[None] * SIDE for _ in range(3)]

    def spread_y(w):
        k = taken[0]
        taken[0] += 1
        mine = pltpu.make_async_copy(piece(w, y), bufs[w].at[y, x], sem.at[k])
        mine.start()
        locals_.append(mine)
        for d in range(1, SIDE):
            first[w][d] = send(piece(w, at(y, d)), bufs[w].at[y, x], dev(dy=d))

    def spread_x(w, d):
        yy = at(y, -d)
        if d == 0:
            src = piece(w, y)
        else:
            first[w][d].wait_recv()
            src = bufs[w].at[yy, x]
        for side, step in enumerate((1, -1)):
            ring[w][d][side] = send(src, bufs[w].at[yy, x], dev(dx=step))

    def pass_on(w, d):
        yy = at(y, -d)
        side, step = (0, 1) if d < 2 else (1, -1)
        ring[w][d][side].wait_recv()
        block = bufs[w].at[yy, at(x, -step)]
        relay[w][d] = send(block, block, dev(dx=step))

    spread_y(0)
    spread_x(0, 0)
    spread_y(1)
    spread_x(1, 0)
    spread_y(2)

    before = (
        lax.broadcasted_iota(jnp.int32, (TOK, TOK), 0) < lax.broadcasted_iota(jnp.int32, (TOK, TOK), 1)
    ).astype(F32).astype(BF)
    ids = ids_ref[...]
    gates = gates_ref[...]
    spot = lax.broadcasted_iota(jnp.int32, (CAP, TOK), 0)
    for e in range(SIDE):
        uses = jnp.where(ids == e, F32(1.0), F32(0.0))
        member = uses[0:1] + uses[1:2]
        weight = uses[0:1] * gates[0:1] + uses[1:2] * gates[1:2]
        place = nn(jnp.broadcast_to(member, (16, TOK)).astype(BF), before)[0:1].astype(jnp.int32)
        hit = jnp.where(spot == place, jnp.broadcast_to(member, (CAP, TOK)), F32(0.0))
        dmat[pl.ds(e * CAP, CAP), :] = hit.astype(BF)
        cmat[pl.ds(e * CAP, CAP), :] = hit * weight
    half = tok_ref[:, pl.ds(pl.multiple_of(c * HALF, HALF), HALF)]
    tsend[...] = nn(dmat[...], half).astype(BF).reshape(SIDE, CAP, HALF)

    def rows_of(block, start=0, size=BLOCK):
        return pl.ds(pl.multiple_of(block * BLOCK + start, 32), size)

    over_z = []
    for d in range(1, SIDE):
        spot_z = pl.ds(pl.multiple_of(y * BLOCK + z * CAP, 32), CAP)
        over_z.append(send(tsend.at[at(z, d)], xs.at[c, spot_z], dev(dz=d)))
    xs[c, pl.ds(pl.multiple_of(y * BLOCK + z * CAP, 32), CAP), :] = tsend[z]

    for d in range(1, SIDE):
        spread_x(0, d)
        if d == 1:
            pass_on(0, 0)
    for copy in over_z:
        copy.wait_recv()
    block = xs.at[c, rows_of(y)]
    up_y = send(block, block, dev(dy=1))
    down_y = send(block, block, dev(dy=-1))
    to_core = [send(block, block, dev(dc=1))]
    pass_on(0, 1)
    pass_on(0, 2)
    pass_on(0, 3)
    for d in range(1, SIDE):
        spread_x(1, d)
    up_y.wait_recv()
    part = xs.at[c, rows_of(at(y, -1), 0, BLOCK // 2)]
    far_a = send(part, part, dev(dy=1))
    block = xs.at[c, rows_of(at(y, -1))]
    to_core.append(send(block, block, dev(dc=1)))
    down_y.wait_recv()
    part = xs.at[c, rows_of(at(y, 1), BLOCK // 2, BLOCK // 2)]
    far_b = send(part, part, dev(dy=-1))
    block = xs.at[c, rows_of(at(y, 1))]
    to_core.append(send(block, block, dev(dc=1)))
    far_a.wait_recv()
    far_b.wait_recv()
    block = xs.at[c, rows_of(at(y, 2))]
    to_core.append(send(block, block, dev(dc=1)))
    for copy in to_core:
        copy.wait_recv()
    for d in range(SIDE):
        pass_on(1, d)
    spread_x(2, 0)
    for d in range(1, SIDE):
        spread_x(2, d)

    def tile(i):
        return pl.ds(pl.multiple_of(i * TILE, TILE), TILE)

    def product(rows, w):
        return nn(xs[0, rows, :], w[0:2].reshape(HALF, FQ)) + nn(xs[1, rows, :], w[2:4].reshape(HALF, FQ))

    def whole(w):
        for d in range(SIDE):
            for side in range(2):
                if (d < 2) != (side == 0):
                    ring[w][d][side].wait_recv()
        for d in range(SIDE):
            relay[w][d].wait_recv()

    @pl.loop(0, ROWS // TILE)
    def _(i):
        rows = tile(i)
        low[rows, :] = (nt(xs[0, rows, :], ain_ref[:, :HALF]) + nt(xs[1, rows, :], ain_ref[:, HALF:])).astype(BF)

    locals_[0].wait()
    whole(0)

    @pl.loop(0, ROWS // TILE)
    def _(i):
        rows = tile(i)
        gate = product(rows, wg)
        act[rows, :] = gate / (1.0 + jnp.exp(-gate))

    aout = aout_ref[:, pl.ds(pl.multiple_of(y * FQ, LANE), FQ)]
    pass_on(2, 0)
    locals_[1].wait()
    whole(1)

    @pl.loop(0, ROWS // TILE)
    def _(i):
        rows = tile(i)
        up = product(rows, wu) + 2.0 * nn(low[rows, :], aout)
        hid[rows, :] = (act[rows, :] * up).astype(BF)

    pass_on(2, 1)

    to_other = [None] * SIDE
    partial = [[None] * SIDE for _ in range(SIDE)]

    def down(g, xx):
        @pl.loop(0, ROWS // TILE)
        def _(i):
            rows = tile(i)
            h = hid[rows, :]
            own[xx, rows, :] = nn(h, jnp.concatenate([wd[2 * c, xx], wd[2 * c + 1, xx]], axis=1))
            o = 1 - c
            oth[xx, rows, :] = nn(h, jnp.concatenate([wd[2 * o, xx], wd[2 * o + 1, xx]], axis=1)).astype(BF)

        to_other[g] = send(oth.at[xx], prt.at[xx], dev(dc=1))

    def scatter(g, xx):
        to_other[g].wait_recv()
        for d in range(SIDE):
            rows = rows_of(at(y, d))
            total = own[xx, rows, :] + prt[xx, rows, :].astype(F32)
            if d == 0:
                own[xx, rows, :] = total
            else:
                rss[xx, rows, :] = total.astype(BF)
                partial[g][d] = send(rss.at[xx, rows], rsr.at[d - 1, xx], dev(dy=d))

    back = []

    def give_back(g, xx):
        total = own[xx, rows_of(y), :]
        for d in range(1, SIDE):
            partial[g][d].wait_recv()
            total = total + rsr[d - 1, xx].astype(F32)
        zs[xx] = total.astype(BF).reshape(SIDE, CAP, 2 * LANE)
        mine = pl.ds(pl.multiple_of(z * CAP, 32), CAP)
        for d in range(1, SIDE):
            back.append(send(zs.at[xx, at(z, d)], ret.at[xx, mine], dev(dz=d)))
        ret[xx, mine, :] = zs[xx, z]

    groups = [x, at(x, -1), at(x, 1), at(x, 2)]
    locals_[2].wait()
    down(0, groups[0])
    pass_on(2, 2)
    pass_on(2, 3)
    ring[2][2][0].wait_recv()
    ring[2][3][0].wait_recv()
    down(1, groups[1])
    scatter(0, groups[0])
    ring[2][0][1].wait_recv()
    ring[2][1][1].wait_recv()
    down(2, groups[2])
    scatter(1, groups[1])
    for d in range(SIDE):
        relay[2][d].wait_recv()
    down(3, groups[3])
    scatter(2, groups[2])
    scatter(3, groups[3])

    copies = (
        lax.rem(lax.broadcasted_iota(jnp.int32, (TAGS, LANE), 1), TAGS)
        == lax.broadcasted_iota(jnp.int32, (TAGS, LANE), 0)
    ).astype(F32).astype(BF)
    tag4[...] = nn(tag_ref[...], copies).astype(BF)
    lane = lax.broadcasted_iota(jnp.int32, (1, LANE), 1)
    head = jnp.zeros((FQ, LANE), F32)
    for a in range(SIDE):
        cols = jnp.concatenate([wd[a, b] for b in range(SIDE)], axis=1)
        head = head + nn(cols, tag4[pl.ds(a * SIDE * LANE, SIDE * LANE), :])
    high, rest = split(head)
    kept = jnp.where(lane < 2 * TAGS, high.astype(F32), rest.astype(F32))
    mp[...] = jnp.where(lane < 3 * TAGS, kept, F32(0.0)).astype(BF)

    for g in range(SIDE):
        give_back(g, groups[g])
    for copy in back:
        copy.wait_recv()

    token_side = cmat[...].T
    c_high, c_rest = split(token_side)
    logits = jnp.zeros((TOK, LANE), F32)
    for b in range(SIDE):
        r = ret[b]
        mix = nn(c_high, r) + nn(c_rest, r)
        for j in range(2):
            cols = pl.ds((SIDE * j + b) * LANE, LANE)
            base = tok_ref[:, pl.ds(pl.multiple_of(c * HALF + (SIDE * j + b) * LANE, LANE), LANE)]
            out = (base.astype(F32) + mix[:, j * LANE : (j + 1) * LANE]).astype(BF)
            layer_ref[:, cols] = out
            head_rows = tag4[pl.ds(pl.multiple_of(c * HALF + (SIDE * j + b) * LANE, LANE), LANE), :]
            logits = logits + nn(out, head_rows)
    lgs[...] = logits
    swap = send(lgs, lgr, dev(dc=1))
    swap.wait_recv()
    logits = lgs[...] + lgr[...]
    grown = jnp.exp(logits)
    total = jnp.sum(jnp.where(lane < TAGS, grown, F32(0.0)), axis=1, keepdims=True)
    hot = lax.rem(lane, TAGS) == labels_ref[...]
    grad = grown / total - jnp.where(hot, F32(1.0), F32(0.0))
    grad = jnp.where(lane < 3 * TAGS, grad, F32(0.0))
    slot = lax.dot_general(
        cmat[...], grad, (((1,), (0,)), ((), ())), preferred_element_type=F32, precision=EXACT
    )
    high, rest = split(slot)
    middle = (lane >= TAGS) & (lane < 2 * TAGS)
    gs[...] = jnp.where(middle, rest.astype(F32), high.astype(F32)).astype(BF).reshape(SIDE, CAP, LANE)

    spot_z = pl.ds(pl.multiple_of(y * BLOCK + z * CAP, 32), CAP)
    grads_z = [send(gs.at[at(z, d)], gx.at[spot_z], dev(dz=d)) for d in range(1, SIDE)]
    gx[spot_z, :] = gs[z]
    for copy in grads_z:
        copy.wait_recv()
    block = gx.at[rows_of(y)]
    grads_y = [send(block, block, dev(dy=d)) for d in range(1, SIDE)]
    for copy in grads_y:
        copy.wait_recv()

    ingp[...] = jnp.zeros_like(ingp)
    ox[x] = jnp.zeros((RANK, FQ), F32)

    @pl.loop(0, ROWS // TILE)
    def _(i):
        rows = tile(i)
        grad_up = (nt(gx[rows, :], mp[...]) * act[rows, :]).astype(BF)
        ox[x] += 2.0 * tn(low[rows, :], grad_up)
        g_high, g_rest = split(2.0 * nt(grad_up, aout))
        for h in range(2):
            ingp[h] += tn(g_high, xs[h, rows, :]) + tn(g_rest, xs[h, rows, :])

    swap = send(ingp.at[1 - c], fp, dev(dc=1))
    outs_x = [send(ox.at[x], ox.at[x], dev(dx=d)) for d in range(1, SIDE)]
    swap.wait_recv()
    fx[x] = ingp[c] + fp[...]
    ins_x = [send(fx.at[x], fx.at[x], dev(dx=d)) for d in range(1, SIDE)]
    for copy in outs_x:
        copy.wait_recv()
    oy[y] = (ox[0] + ox[1]) + (ox[2] + ox[3])
    outs_y = [send(oy.at[y], oy.at[y], dev(dy=d)) for d in range(1, SIDE)]
    for copy in ins_x:
        copy.wait_recv()
    fy[y] = (fx[0] + fx[1]) + (fx[2] + fx[3])
    ins_y = [send(fy.at[y], fy.at[y], dev(dy=d)) for d in range(1, SIDE)]
    for copy in outs_y:
        copy.wait_recv()
    for a in range(SIDE):
        outg_ref[:, pl.ds(a * FQ, FQ)] = oy[a]
    for copy in ins_y:
        copy.wait_recv()
    fx_sum = (fy[0] + fy[1]) + (fy[2] + fy[3])
    done[c] = fx_sum
    swap = send(done.at[c], done.at[c], dev(dc=1))
    swap.wait_recv()
    ing_ref[:, :HALF] = done[0]
    ing_ref[:, HALF:] = done[1]
    for copy in sent:
        copy.wait_send()


def local(tokens, expert_ids, gate_values, tag_labels, w_gate, w_up, w_down, adapter_in, adapter_out, tag_weight):
    vmem = pl.BlockSpec(memory_space=pltpu.VMEM)
    hbm = pl.BlockSpec(memory_space=pl.ANY)
    layer, in_grad, out_grad = pl.pallas_call(
        kernel,
        out_shape=(
            jax.ShapeDtypeStruct((TOK, HALF), BF),
            jax.ShapeDtypeStruct((RANK, DIM), F32),
            jax.ShapeDtypeStruct((RANK, SHARD), F32),
        ),
        in_specs=[vmem] * 7 + [hbm] * 3,
        out_specs=(vmem, vmem, vmem),
        scratch_shapes=[
            pltpu.VMEM((SIDE, SIDE, LANE, FQ), BF),
            pltpu.VMEM((SIDE, SIDE, LANE, FQ), BF),
            pltpu.VMEM((SIDE, SIDE, FQ, LANE), BF),
            pltpu.VMEM((SIDE, CAP, HALF), BF),
            pltpu.VMEM((2, ROWS, HALF), BF),
            pltpu.VMEM((ROWS, FQ), F32),
            pltpu.VMEM((ROWS, FQ), BF),
            pltpu.VMEM((ROWS, RANK), BF),
            pltpu.VMEM((BLOCK, TOK), BF),
            pltpu.VMEM((BLOCK, TOK), F32),
            pltpu.VMEM((SIDE, ROWS, 2 * LANE), F32),
            pltpu.VMEM((SIDE, ROWS, 2 * LANE), BF),
            pltpu.VMEM((SIDE, ROWS, 2 * LANE), BF),
            pltpu.VMEM((SIDE, ROWS, 2 * LANE), BF),
            pltpu.VMEM((SIDE - 1, SIDE, BLOCK, 2 * LANE), BF),
            pltpu.VMEM((SIDE, SIDE, CAP, 2 * LANE), BF),
            pltpu.VMEM((SIDE, BLOCK, 2 * LANE), BF),
            pltpu.VMEM((TOK, LANE), F32),
            pltpu.VMEM((TOK, LANE), F32),
            pltpu.VMEM((DIM, LANE), BF),
            pltpu.VMEM((FQ, LANE), BF),
            pltpu.VMEM((SIDE, CAP, LANE), BF),
            pltpu.VMEM((ROWS, LANE), BF),
            pltpu.VMEM((2, RANK, HALF), F32),
            pltpu.VMEM((RANK, HALF), F32),
            pltpu.VMEM((SIDE, RANK, HALF), F32),
            pltpu.VMEM((SIDE, RANK, FQ), F32),
            pltpu.VMEM((SIDE, RANK, HALF), F32),
            pltpu.VMEM((SIDE, RANK, FQ), F32),
            pltpu.VMEM((2, RANK, HALF), F32),
            pltpu.SemaphoreType.DMA((256,)),
        ],
        compiler_params=pltpu.CompilerParams(
            collective_id=0, has_side_effects=True, vmem_limit_bytes=62 * 1024 * 1024
        ),
    )(
        expert_ids.T, gate_values.T, tag_labels.reshape(TOK, 1), tokens,
        adapter_in[0], adapter_out[0], tag_weight, w_gate, w_up, w_down,
    )
    return layer, in_grad[None], out_grad[None]


def solution(mesh):
    in_specs = (
        P(("dp", "expert"), None),
        P(("dp", "expert"), None),
        P(("dp", "expert"), None),
        P(("dp", "expert")),
        P("expert", "dp", "tensor"),
        P("expert", "dp", "tensor"),
        P("expert", "tensor", "dp"),
        P("expert", None, None),
        P("expert", None, "tensor"),
        P(),
    )
    out_specs = (
        P(("dp", "expert"), "tensor"),
        P("expert", None, None),
        P("expert", None, "tensor"),
    )
    return jax.shard_map(local, mesh=mesh, in_specs=in_specs, out_specs=out_specs, check_vma=False)
```

time: 611 us -> 188 us (0.31)
  waiting for transfers between devices: 460 us -> 0 us
  Pallas kernels: 0 us -> 180 us
  blocking collectives: 64 us -> 0 us
  matrix products: 58.3 us -> 0 us
  between operations: 13.9 us -> 0.66 us
    all_gather x3 -> x0, waiting for transfers between devices: 262 us -> none  [the longest x1 98.6 us: local(): down_full = lax.all_gather(w_down, 'dp', axis=2, tiled=True)[0]]
    pallas_call x0 -> x1, Pallas kernels: none -> 180 us  [local(): pl.pallas_call(kernel, out_shape=(jax.ShapeDtypeStruct((TOK, HALF), BF),...]
    psum x2 -> x0, waiting for transfers between devices: 176 us -> none  [the longest x1 94.4 us: local(): lax.psum(in_local.astype(jnp.bfloat16), ('dp', 'tensor'))]
    dot_general x13 -> x0, matrix products: 58.3 us -> none  [the longest x1 15.2 us: local(): jnp.dot(hidden, down_full, preferred_element_type=jnp.float32)]
    all_to_all x2 -> x0, blocking collectives: 49.8 us -> none  [the longest x1 25.5 us: local(): lax.all_to_all(outgoing.reshape(experts, capacity, model_width), 'expert'...]
    all_to_all x1 -> x0, waiting for transfers between devices: 19.5 us -> none  [local(): lax.all_to_all(slot_out.reshape(experts, capacity, model_width), 'expert'...]
    psum x1 -> x0, blocking collectives: 14.1 us -> none  [local(): summed = lax.psum(partial_value, 'tensor').astype(jnp.bfloat16)]
  transfers between devices with their start and end apart: 6 -> 0, of which waited for: 6 -> 0; matrix products, arithmetic and copies ran while one was open for 5% -> 0% of each run, Pallas kernels for 0% -> 0%
where the time goes in v1:
time: 188 us
  Pallas kernels  180 us (96%)
  local copies, waits for them, and re-layouts  6.67 us (4%)
    pallas_call x1, Pallas kernels, local(): pl.pallas_call(kernel, out_shape=(jax.ShapeDtypeStruct((TOK, HALF), BF),...  180 us
    unnamed x10, local copies, waits for them, and re-layouts  5.93 us

profile of v1, /device:TPU:1, one launch (start us, length us, event | category | flops | bytes accessed | tf_op | source)
XLA Modules:
  0.0 187.7 jit_solution(4841097073634493677)
XLA Ops:
  0.6 0.0 copy-start.2
  0.6 0.6 copy-done.2
  1.3 0.7 copy.13.labels_ref
  2.0 1.9 %copy.14.tag_ref = bf16[2048,32]{1,0:T(8,128)(2,1)} copy(bf16[2048,32]{0,1:T(8,128)(2,1)} %param.19) | data formatting | bytes 262144 | tf_op args[9]
  3.9 180.4 %shard_map.121 = (bf16[128,1024]{1,0:T(8,128)(2,1)}, f32[16,2048]{1,0:T(8,128)}, f32[16,3584]{1,0:T(8,128)}) custom-call(s32[2,128]{1,0:T(2,128)} %bitcast.11, f32[2,128]{1,0:T(2,128)} %bitcast.12, s32[128,1]{1,0:T(8,128)} %copy.13.labels_ref, bf16[128,2048]{1,0:T(8,128)(2,1)} %tok_ref.1, bf16[16,2048]{1,0:T(8,128)(2,1)} %bitcast.10, ...), custom_call_target="tpu_custom_call" | custom-call | tf_op jit(solution)/shard_map/pallas_call | solution.py:397
  184.3 0.0 copy-start.1
  184.3 1.7 copy.18
  186.0 0.0 copy-done.1
  186.0 0.0 copy-start
  186.0 0.7 copy.19
  186.7 0.3 copy-done
  187.0 0.7 copy.20
Async XLA Ops:
  0.6 0.7 copy-start.2
  184.3 1.7 copy-start.1
  186.0 1.0 copy-start

commit v2 on v1

--- a/solution.py
+++ b/solution.py
@@ -21,6 +21,7 @@
 TOK = 128
 CAP = 96
 BLOCK = SIDE * CAP
+MID = BLOCK // 2
 ROWS = SIDE * BLOCK
 TILE = 512
 
@@ -35,6 +36,10 @@
 
 def tn(a, b):
     return lax.dot_general(a, b, (((0,), (0,)), ((), ())), preferred_element_type=F32)
+
+
+def four(ref):
+    return (ref[0].astype(F32) + ref[1].astype(F32)) + (ref[2].astype(F32) + ref[3].astype(F32))
 
 
 def split(v):
@@ -46,7 +51,7 @@
     ids_ref, gates_ref, labels_ref, tok_ref, ain_ref, aout_ref, tag_ref, wg_hbm, wu_hbm, wd_hbm,
     layer_ref, ing_ref, outg_ref,
     wg, wu, wd, tsend, xs, act, hid, low, dmat, cmat, own, oth, prt, rss, rsr, zs, ret,
-    lgs, lgr, tag4, mp, gs, gx, ingp, fp, fx, ox, fy, oy, done, sem,
+    lgs, lgr, tag4, mp, gs, gx, ingp, fp, fx, ox, fy, oy, done, oacc, sem,
 ):
     me = lax.axis_index("dp")
     y = me // SIDE
@@ -234,9 +239,11 @@
         hid[rows, :] = (act[rows, :] * up).astype(BF)
 
     pass_on(2, 1)
+    pass_on(2, 2)
 
     to_other = [None] * SIDE
-    partial = [[None] * SIDE for _ in range(SIDE)]
+    far = [[None, None] for _ in range(SIDE)]
+    near = [[] for _ in range(SIDE)]
 
     def down(g, xx):
         @pl.loop(0, ROWS // TILE)
@@ -249,24 +256,44 @@
 
         to_other[g] = send(oth.at[xx], prt.at[xx], dev(dc=1))
 
+    first_half = pl.ds(0, MID)
+    last_half = pl.ds(MID, MID)
+
     def scatter(g, xx):
         to_other[g].wait_recv()
-        for d in range(SIDE):
-            rows = rows_of(at(y, d))
-            total = own[xx, rows, :] + prt[xx, rows, :].astype(F32)
-            if d == 0:
-                own[xx, rows, :] = total
-            else:
-                rss[xx, rows, :] = total.astype(BF)
-                partial[g][d] = send(rss.at[xx, rows], rsr.at[d - 1, xx], dev(dy=d))
+
+        def total(rows):
+            return own[xx, rows, :] + prt[xx, rows, :].astype(F32)
+
+        low_rows = rows_of(at(y, 2), 0, MID)
+        rss[xx, low_rows, :] = total(low_rows).astype(BF)
+        far[g][0] = send(rss.at[xx, low_rows], rsr.at[1, xx, first_half], dev(dy=1))
+        high_rows = rows_of(at(y, 2), MID, MID)
+        rss[xx, high_rows, :] = total(high_rows).astype(BF)
+        far[g][1] = send(rss.at[xx, high_rows], rsr.at[1, xx, last_half], dev(dy=-1))
+        rows = rows_of(at(y, 1), MID, MID)
+        rss[xx, rows, :] = total(rows).astype(BF)
+        near[g].append(send(rss.at[xx, rows], rsr.at[0, xx, last_half], dev(dy=1)))
+        rows = rows_of(at(y, -1), 0, MID)
+        rss[xx, rows, :] = total(rows).astype(BF)
+        near[g].append(send(rss.at[xx, rows], rsr.at[2, xx, first_half], dev(dy=-1)))
+
+    def merge(g, xx):
+        for side, step in enumerate((1, -1)):
+            rows = rows_of(at(y, step), side * MID, MID)
+            half = (first_half, last_half)[side]
+            mine = own[xx, rows, :] + prt[xx, rows, :].astype(F32)
+            far[g][side].wait_recv()
+            rss[xx, rows, :] = (mine + rsr[1, xx, half, :].astype(F32)).astype(BF)
+            near[g].append(send(rss.at[xx, rows], rsr.at[2 * side, xx, half], dev(dy=step)))
 
     back = []
 
     def give_back(g, xx):
-        total = own[xx, rows_of(y), :]
-        for d in range(1, SIDE):
-            partial[g][d].wait_recv()
-            total = total + rsr[d - 1, xx].astype(F32)
+        total = own[xx, rows_of(y), :] + prt[xx, rows_of(y), :].astype(F32)
+        for copy in near[g]:
+            copy.wait_recv()
+        total = total + rsr[0, xx].astype(F32) + rsr[2, xx].astype(F32)
         zs[xx] = total.astype(BF).reshape(SIDE, CAP, 2 * LANE)
         mine = pl.ds(pl.multiple_of(z * CAP, 32), CAP)
         for d in range(1, SIDE):
@@ -276,7 +303,6 @@
     groups = [x, at(x, -1), at(x, 1), at(x, 2)]
     locals_[2].wait()
     down(0, groups[0])
-    pass_on(2, 2)
     pass_on(2, 3)
     ring[2][2][0].wait_recv()
     ring[2][3][0].wait_recv()
@@ -286,11 +312,17 @@
     ring[2][1][1].wait_recv()
     down(2, groups[2])
     scatter(1, groups[1])
+    merge(0, groups[0])
     for d in range(SIDE):
         relay[2][d].wait_recv()
     down(3, groups[3])
     scatter(2, groups[2])
+    merge(1, groups[1])
     scatter(3, groups[3])
+    merge(2, groups[2])
+    give_back(0, groups[0])
+    merge(3, groups[3])
+    give_back(1, groups[1])
 
     copies = (
         lax.rem(lax.broadcasted_iota(jnp.int32, (TAGS, LANE), 1), TAGS)
@@ -306,7 +338,7 @@
     kept = jnp.where(lane < 2 * TAGS, high.astype(F32), rest.astype(F32))
     mp[...] = jnp.where(lane < 3 * TAGS, kept, F32(0.0)).astype(BF)
 
-    for g in range(SIDE):
+    for g in range(2, SIDE):
         give_back(g, groups[g])
     for copy in back:
         copy.wait_recv()
@@ -351,38 +383,38 @@
         copy.wait_recv()
 
     ingp[...] = jnp.zeros_like(ingp)
-    ox[x] = jnp.zeros((RANK, FQ), F32)
+    oacc[...] = jnp.zeros_like(oacc)
 
     @pl.loop(0, ROWS // TILE)
     def _(i):
         rows = tile(i)
         grad_up = (nt(gx[rows, :], mp[...]) * act[rows, :]).astype(BF)
-        ox[x] += 2.0 * tn(low[rows, :], grad_up)
-        g_high, g_rest = split(2.0 * nt(grad_up, aout))
+        oacc[...] += 2.0 * tn(low[rows, :], grad_up)
+        low_grad = (2.0 * nt(grad_up, aout)).astype(BF)
         for h in range(2):
-            ingp[h] += tn(g_high, xs[h, rows, :]) + tn(g_rest, xs[h, rows, :])
+            ingp[h] += tn(low_grad, xs[h, rows, :])
 
     swap = send(ingp.at[1 - c], fp, dev(dc=1))
+    ox[x] = oacc[...].astype(BF)
     outs_x = [send(ox.at[x], ox.at[x], dev(dx=d)) for d in range(1, SIDE)]
     swap.wait_recv()
-    fx[x] = ingp[c] + fp[...]
+    fx[x] = (ingp[c] + fp[...]).astype(BF)
     ins_x = [send(fx.at[x], fx.at[x], dev(dx=d)) for d in range(1, SIDE)]
     for copy in outs_x:
         copy.wait_recv()
-    oy[y] = (ox[0] + ox[1]) + (ox[2] + ox[3])
+    oy[y] = four(ox).astype(BF)
     outs_y = [send(oy.at[y], oy.at[y], dev(dy=d)) for d in range(1, SIDE)]
     for copy in ins_x:
         copy.wait_recv()
-    fy[y] = (fx[0] + fx[1]) + (fx[2] + fx[3])
+    fy[y] = four(fx).astype(BF)
     ins_y = [send(fy.at[y], fy.at[y], dev(dy=d)) for d in range(1, SIDE)]
     for copy in outs_y:
         copy.wait_recv()
     for a in range(SIDE):
-        outg_ref[:, pl.ds(a * FQ, FQ)] = oy[a]
+        outg_ref[:, pl.ds(a * FQ, FQ)] = oy[a].astype(F32)
     for copy in ins_y:
         copy.wait_recv()
-    fx_sum = (fy[0] + fy[1]) + (fy[2] + fy[3])
-    done[c] = fx_sum
+    done[c] = four(fy)
     swap = send(done.at[c], done.at[c], dev(dc=1))
     swap.wait_recv()
     ing_ref[:, :HALF] = done[0]
@@ -429,12 +461,13 @@
             pltpu.VMEM((ROWS, LANE), BF),
             pltpu.VMEM((2, RANK, HALF), F32),
             pltpu.VMEM((RANK, HALF), F32),
-            pltpu.VMEM((SIDE, RANK, HALF), F32),
-            pltpu.VMEM((SIDE, RANK, FQ), F32),
-            pltpu.VMEM((SIDE, RANK, HALF), F32),
-            pltpu.VMEM((SIDE, RANK, FQ), F32),
+            pltpu.VMEM((SIDE, RANK, HALF), BF),
+            pltpu.VMEM((SIDE, RANK, FQ), BF),
+            pltpu.VMEM((SIDE, RANK, HALF), BF),
+            pltpu.VMEM((SIDE, RANK, FQ), BF),
             pltpu.VMEM((2, RANK, HALF), F32),
-            pltpu.SemaphoreType.DMA((256,)),
+            pltpu.VMEM((RANK, FQ), F32),
+            pltpu.SemaphoreType.DMA((320,)),
         ],
         compiler_params=pltpu.CompilerParams(
             collective_id=0, has_side_effects=True, vmem_limit_bytes=62 * 1024 * 1024

time: 188 us -> 174 us (0.926)
  Pallas kernels: 180 us -> 167 us
    pallas_call x1, Pallas kernels: 180 us -> 167 us  [local(): pl.pallas_call(kernel, out_shape=(jax.ShapeDtypeStruct((TOK, HALF), BF),...]
where the time goes in v2:
time: 174 us
  Pallas kernels  167 us (96%)
  local copies, waits for them, and re-layouts  6.67 us (4%)
    pallas_call x1, Pallas kernels, local(): pl.pallas_call(kernel, out_shape=(jax.ShapeDtypeStruct((TOK, HALF), BF),...  167 us
    unnamed x10, local copies, waits for them, and re-layouts  5.93 us

profile of v2, /device:TPU:1, one launch (start us, length us, event | category | flops | bytes accessed | tf_op | source)
XLA Modules:
  0.0 174.2 jit_solution(7445224524914501580)
XLA Ops:
  0.6 0.0 copy-start.2
  0.6 0.6 copy-done.2
  1.3 0.7 copy.13.labels_ref
  2.0 1.9 %copy.14.tag_ref = bf16[2048,32]{1,0:T(8,128)(2,1)} copy(bf16[2048,32]{0,1:T(8,128)(2,1)} %param.19) | data formatting | bytes 262144 | tf_op args[9]
  3.9 166.9 %shard_map.121 = (bf16[128,1024]{1,0:T(8,128)(2,1)}, f32[16,2048]{1,0:T(8,128)}, f32[16,3584]{1,0:T(8,128)}) custom-call(s32[2,128]{1,0:T(2,128)} %bitcast.11, f32[2,128]{1,0:T(2,128)} %bitcast.12, s32[128,1]{1,0:T(8,128)} %copy.13.labels_ref, bf16[128,2048]{1,0:T(8,128)(2,1)} %tok_ref.1, bf16[16,2048]{1,0:T(8,128)(2,1)} %bitcast.10, ...), custom_call_target="tpu_custom_call" | custom-call | tf_op jit(solution)/shard_map/pallas_call | solution.py:429
  170.8 0.0 copy-start.1
  170.8 1.7 copy.18
  172.5 0.0 copy-done.1
  172.5 0.0 copy-start
  172.5 0.7 copy.19
  173.2 0.3 copy-done
  173.5 0.7 copy.20
Async XLA Ops:
  0.6 0.7 copy-start.2
  170.8 1.7 copy-start.1
  172.5 1.0 copy-start

commit v3 on v2

--- a/solution.py
+++ b/solution.py
@@ -134,7 +134,6 @@
     spread_x(0, 0)
     spread_y(1)
     spread_x(1, 0)
-    spread_y(2)
 
     before = (
         lax.broadcasted_iota(jnp.int32, (TOK, TOK), 0) < lax.broadcasted_iota(jnp.int32, (TOK, TOK), 1)
@@ -185,19 +184,18 @@
     down_y.wait_recv()
     part = xs.at[c, rows_of(at(y, 1), BLOCK // 2, BLOCK // 2)]
     far_b = send(part, part, dev(dy=-1))
+    spread_y(2)
     block = xs.at[c, rows_of(at(y, 1))]
     to_core.append(send(block, block, dev(dc=1)))
+    for d in range(SIDE):
+        pass_on(1, d)
+    spread_x(2, 0)
     far_a.wait_recv()
     far_b.wait_recv()
     block = xs.at[c, rows_of(at(y, 2))]
     to_core.append(send(block, block, dev(dc=1)))
     for copy in to_core:
         copy.wait_recv()
-    for d in range(SIDE):
-        pass_on(1, d)
-    spread_x(2, 0)
-    for d in range(1, SIDE):
-        spread_x(2, d)
 
     def tile(i):
         return pl.ds(pl.multiple_of(i * TILE, TILE), TILE)
@@ -228,7 +226,8 @@
         act[rows, :] = gate / (1.0 + jnp.exp(-gate))
 
     aout = aout_ref[:, pl.ds(pl.multiple_of(y * FQ, LANE), FQ)]
-    pass_on(2, 0)
+    for d in range(1, SIDE):
+        spread_x(2, d)
     locals_[1].wait()
     whole(1)
 
@@ -238,8 +237,8 @@
         up = product(rows, wu) + 2.0 * nn(low[rows, :], aout)
         hid[rows, :] = (act[rows, :] * up).astype(BF)
 
-    pass_on(2, 1)
-    pass_on(2, 2)
+    for d in range(3):
+        pass_on(2, d)
 
     to_other = [None] * SIDE
     far = [[None, None] for _ in range(SIDE)]

time: 174 us -> 165 us (0.948)
  Pallas kernels: 167 us -> 157 us
    pallas_call x1, Pallas kernels: 167 us -> 157 us  [local(): pl.pallas_call(kernel, out_shape=(jax.ShapeDtypeStruct((TOK, HALF), BF),...]
where the time goes in v3:
time: 165 us
  Pallas kernels  157 us (95%)
  local copies, waits for them, and re-layouts  6.67 us (4%)
    pallas_call x1, Pallas kernels, local(): pl.pallas_call(kernel, out_shape=(jax.ShapeDtypeStruct((TOK, HALF), BF),...  157 us
    unnamed x10, local copies, waits for them, and re-layouts  5.93 us

profile of v3, /device:TPU:1, one launch (start us, length us, event | category | flops | bytes accessed | tf_op | source)
XLA Modules:
  0.0 164.6 jit_solution(13237684210698004324)
XLA Ops:
  0.6 0.0 copy-start.2
  0.6 0.6 copy-done.2
  1.3 0.7 copy.13.labels_ref
  2.0 1.9 %copy.14.tag_ref = bf16[2048,32]{1,0:T(8,128)(2,1)} copy(bf16[2048,32]{0,1:T(8,128)(2,1)} %param.19) | data formatting | bytes 262144 | tf_op args[9]
  3.9 157.2 %shard_map.121 = (bf16[128,1024]{1,0:T(8,128)(2,1)}, f32[16,2048]{1,0:T(8,128)}, f32[16,3584]{1,0:T(8,128)}) custom-call(s32[2,128]{1,0:T(2,128)} %bitcast.11, f32[2,128]{1,0:T(2,128)} %bitcast.12, s32[128,1]{1,0:T(8,128)} %copy.13.labels_ref, bf16[128,2048]{1,0:T(8,128)(2,1)} %tok_ref.1, bf16[16,2048]{1,0:T(8,128)(2,1)} %bitcast.10, ...), custom_call_target="tpu_custom_call" | custom-call | tf_op jit(solution)/shard_map/pallas_call | solution.py:428
  161.2 0.0 copy-start.1
  161.2 1.7 %copy.18 = bf16[128,1024]{1,0:T(8,128)(2,1)} copy(bf16[128,1024]{1,0:T(8,128)(2,1)} %get-tuple-element.12) | data formatting | bytes 524288
  162.9 0.0 copy-done.1
  162.9 0.0 copy-start
  162.9 0.7 copy.19
  163.6 0.3 copy-done
  163.9 0.7 copy.20
Async XLA Ops:
  0.6 0.7 copy-start.2
  161.2 1.7 %copy-start.1 = (f32[16,2048]{1,0:T(8,128)S(1)}, f32[16,2048]{1,0:T(8,128)}, u32[]{:S(2)}) copy-start(f32[16,2048]{1,0:T(8,128)} %get-tuple-element.7) | copy-start | bytes 393220
  162.9 1.0 copy-start

commit v4 on v3

--- a/solution.py
+++ b/solution.py
@@ -378,15 +378,14 @@
         copy.wait_recv()
     block = gx.at[rows_of(y)]
     grads_y = [send(block, block, dev(dy=d)) for d in range(1, SIDE)]
-    for copy in grads_y:
-        copy.wait_recv()
 
     ingp[...] = jnp.zeros_like(ingp)
     oacc[...] = jnp.zeros_like(oacc)
 
-    @pl.loop(0, ROWS // TILE)
-    def _(i):
-        rows = tile(i)
+    for d in (0, 1, 3, 2):
+        if d:
+            grads_y[d - 1].wait_recv()
+        rows = rows_of(at(y, -d))
         grad_up = (nt(gx[rows, :], mp[...]) * act[rows, :]).astype(BF)
         oacc[...] += 2.0 * tn(low[rows, :], grad_up)
         low_grad = (2.0 * nt(grad_up, aout)).astype(BF)

time: 165 us -> 163 us (0.988)
  Pallas kernels: 157 us -> 155 us
    pallas_call x1, Pallas kernels: 157 us -> 155 us  [local(): pl.pallas_call(kernel, out_shape=(jax.ShapeDtypeStruct((TOK, HALF), BF),...]
where the time goes in v4:
time: 163 us
  Pallas kernels  155 us (95%)
  local copies, waits for them, and re-layouts  6.67 us (4%)
    pallas_call x1, Pallas kernels, local(): pl.pallas_call(kernel, out_shape=(jax.ShapeDtypeStruct((TOK, HALF), BF),...  155 us
    unnamed x10, local copies, waits for them, and re-layouts  5.93 us

profile of v4, /device:TPU:1, one launch (start us, length us, event | category | flops | bytes accessed | tf_op | source)
XLA Modules:
  0.0 162.7 jit_solution(4793066478316640697)
XLA Ops:
  0.6 0.0 copy-start.2
  0.6 0.6 copy-done.2
  1.3 0.7 copy.13.labels_ref
  2.0 1.9 %copy.14.tag_ref = bf16[2048,32]{1,0:T(8,128)(2,1)} copy(bf16[2048,32]{0,1:T(8,128)(2,1)} %param.19) | data formatting | bytes 262144 | tf_op args[9]
  3.9 155.3 %shard_map.121 = (bf16[128,1024]{1,0:T(8,128)(2,1)}, f32[16,2048]{1,0:T(8,128)}, f32[16,3584]{1,0:T(8,128)}) custom-call(s32[2,128]{1,0:T(2,128)} %bitcast.11, f32[2,128]{1,0:T(2,128)} %bitcast.12, s32[128,1]{1,0:T(8,128)} %copy.13.labels_ref, bf16[128,2048]{1,0:T(8,128)(2,1)} %tok_ref.1, bf16[16,2048]{1,0:T(8,128)(2,1)} %bitcast.10, ...), custom_call_target="tpu_custom_call" | custom-call | tf_op jit(solution)/shard_map/pallas_call | solution.py:427
  159.3 0.0 copy-start.1
  159.3 1.7 %copy.18 = bf16[128,1024]{1,0:T(8,128)(2,1)} copy(bf16[128,1024]{1,0:T(8,128)(2,1)} %get-tuple-element.12) | data formatting | bytes 524288
  161.0 0.0 copy-done.1
  161.0 0.0 copy-start
  161.0 0.7 copy.19
  161.7 0.3 copy-done
  162.0 0.7 copy.20
Async XLA Ops:
  0.6 0.7 copy-start.2
  159.3 1.7 %copy-start.1 = (f32[16,2048]{1,0:T(8,128)S(1)}, f32[16,2048]{1,0:T(8,128)}, u32[]{:S(2)}) copy-start(f32[16,2048]{1,0:T(8,128)} %get-tuple-element.7) | copy-start | bytes 393220
  161.0 1.0 copy-start
